TPU v7x, 32 devices: a whole 2x2x4 slice. The times are simulated.
32 devices in a mesh: tm: 8 (over z, x), space: 4 (over y, core).
Axes of the slice: x: 2, y: 2, z: 4, core: 2. Of those that a mesh axis runs over, the one named last changes fastest.
Arguments:
- guess: float32 [8, 1, 64, 4096], P('tm', None, None, 'space'), may hold values from -6 to 6
- kernels: bfloat16 [16, 64, 576], P('tm'), may hold values from -0.25 to 0.25
- biases: float32 [16, 64], P('tm'), may hold values from -6 to 6
- probes: bfloat16 [2, 1, 64, 4096], P(None, None, None, 'space'), may hold values from -6 to 6
Outputs:
- states: float32 [8, 1, 64, 4096], P('tm', None, None, 'space')
- log_change: float32 [16], P('tm')
All inputs are finite; a program needn't handle non-finite values.
Results may differ from a plain program's by a relative error of at most 0.0018.
Values may be sent and summed in bfloat16 or wider, within the bound.
A program may use at most 128 MiB of HBM per device.

v0:
```python
import jax
import jax.numpy as jnp
from jax import lax
from jax.sharding import PartitionSpec as P

WIDTH = 64


step_size = 0.0078125
highest = lax.Precision.HIGHEST


def extended(block, sides, width):
    for axis, dim in sides:
        count = lax.axis_size(axis)
        forward = [(i, i + 1) for i in range(count - 1)]
        backward = [(target, source) for source, target in forward]
        low = lax.ppermute(
            lax.slice_in_dim(block, block.shape[dim] - width, None, axis=dim), axis, forward
        )
        high = lax.ppermute(lax.slice_in_dim(block, 0, width, axis=dim), axis, backward)
        block = jnp.concatenate([low, block, high], axis=dim)
    return block


def carried_in(shard, axis, combine, identity):
    peers, index = (lax.axis_size(axis), lax.axis_index(axis))
    everything = jax.tree.map(lambda part: lax.all_gather(part, axis), shard)
    start = jax.tree.map(
        lambda part, zero: jnp.broadcast_to(jnp.asarray(zero, part.dtype), part.shape),
        shard,
        identity,
    )

    def turn(k, before):
        reached = k < index
        new = combine(before, jax.tree.map(lambda part: part[k], everything))
        return jax.tree.map(lambda a, b: jnp.where(reached, a, b), new, before)

    return lax.fori_loop(0, peers, turn, start)


def gather_taps(stacked, row_len):
    out_rows = stacked.shape[2] // row_len - 2
    out_cells = out_rows * row_len
    padded = jnp.pad(stacked, ((0, 0), (0, 0), (1, 1)))
    column = jnp.arange(out_cells, dtype=jnp.int32) % row_len
    pieces = []
    for row_off in (-1, 0, 1):
        for col_off in (-1, 0, 1):
            offset = (1 + row_off) * row_len + col_off + 1
            window = padded[:, :, offset : offset + out_cells]
            if col_off == -1:
                window = jnp.where(column != 0, window, jnp.zeros_like(window))
            elif col_off == 1:
                window = jnp.where(column != row_len - 1, window, jnp.zeros_like(window))
            pieces.append(window)
    return jnp.concatenate(pieces, axis=1)


def mix_channels(matrix, field):
    return jnp.einsum("ij,bjn->bin", matrix, field, precision=highest)


def compose(earlier, later):
    return (
        jnp.dot(later[0], earlier[0], precision=highest),
        mix_channels(later[0], earlier[1]) + later[1],
    )


def accumulate(earlier, later):
    return earlier + later


def body(guess, kernels, biases, probes):
    row_len = WIDTH
    cells = guess.shape[3]
    images = guess.shape[1]
    rows = cells // row_len
    layers = kernels.shape[0]
    channels = kernels.shape[1]
    probe_count = probes.shape[0]
    strip = lax.axis_index("space")
    strips = lax.axis_size("space")
    position = lax.axis_index("tm")
    probe_ext = extended(probes, (("space", 3),), layers * row_len)
    probe_mid = probe_ext[:, :, :, layers * row_len : (layers + rows) * row_len].astype(jnp.float32)
    current = extended(guess[0], (("space", 2),), layers * row_len)
    partials = []
    for layer_index in range(layers):
        extent = layers - layer_index
        widened = current
        ext_cells = (rows + 2 * extent) * row_len
        global_row = strip * rows + jnp.arange(ext_cells, dtype=jnp.int32) // row_len - extent
        inside = (global_row >= 0) & (global_row < rows * strips)
        activation = jnp.where(inside, jnp.tanh(widened), 0.0)
        slopes = 1.0 - activation * activation
        start_cell = (layers - extent) * row_len
        probe_win = lax.slice_in_dim(probe_ext, start_cell, start_cell + ext_cells, axis=3).astype(
            jnp.float32
        )
        inputs = jnp.concatenate(
            [activation[0][None], slopes[0][None] * probe_win[:, 0]], axis=0
        ).astype(jnp.bfloat16)
        stacked = gather_taps(inputs, row_len)
        mixing = jnp.einsum(
            "ok,skn->son", kernels[layer_index], stacked, preferred_element_type=jnp.float32
        )
        forcing = mixing[0] + biases[layer_index][:, None]
        advanced = [widened[0, :, row_len : ext_cells - row_len] + step_size * forcing]
        inner = mixing[1:, :, (extent - 1) * row_len : (extent - 1 + rows) * row_len]
        partial_value = jnp.sum(probe_mid[:, 0] * inner)
        current = jnp.stack(advanced)
        partial_value = partial_value / (probe_count * images)
        partial_value = lax.psum(partial_value, "space")
        partials.append(partial_value)
    traces = jnp.stack(partials)
    kernel_sum = kernels.astype(jnp.float32).reshape(layers, channels, 9, channels).sum(axis=(0, 2))
    identity = jnp.eye(channels, dtype=jnp.float32)
    matrix = identity + step_size * kernel_sum
    leading = position == 0
    offset = current - mix_channels(matrix, guess[0])
    matrix_elem = jnp.where(leading, 0.0, matrix)
    offset_elem = jnp.where(leading, current, offset)
    prefix_matrix, prefix_offset = carried_in(
        (matrix_elem, offset_elem), "tm", compose, (identity, jnp.zeros_like(current))
    )
    new_state = mix_channels(prefix_matrix, guess[0]) + prefix_offset
    earlier_total = carried_in(jnp.sum(traces), "tm", accumulate, jnp.zeros((), jnp.float32))
    log_change = -(step_size / row_len) * (earlier_total + jnp.cumsum(traces))
    return (new_state[None], log_change)


def solution(mesh):
    return jax.shard_map(
        body,
        mesh=mesh,
        in_specs=(
            P("tm", None, None, "space"),
            P("tm", None, None),
            P("tm", None),
            P(None, None, None, "space"),
        ),
        out_specs=(P("tm", None, None, "space"), P("tm")),
        check_vma=False,
    )
```

profile of v0, /device:TPU:0, one launch (start us, length us, event | category | flops | bytes accessed | tf_op | source)
XLA Modules:
  0.0 128.0 jit_solution(14114822554420706870)
XLA Ops:
  8.0 2.4 %collective-permute-start = (f32[1,64,128]{2,1,0:T(8,128)S(1)}, f32[1,64,128]{2,1,0:T(8,128)S(1)}, u32[]{:S(2)}, u32[]{:S(2)}) collective-permute-start(f32[1,64,128]{2,1,0:T(8,128)S(1)} %get-tuple-element.263), channel_id=1, source_target_pairs={{0,1},{1,2},{2,3},{4,5},{5,6},{6,7},{8,9},{9,10},{10,11},{12,13},{... | collective-permute-start | bytes 98312 | tf_op jit(solution)/shard_map/ppermute | solution.py:18
  10.4 1.3 %collective-permute-start.1 = (f32[1,64,128]{2,1,0:T(8,128)S(1)}, f32[1,64,128]{2,1,0:T(8,128)S(1)}, u32[]{:S(2)}, u32[]{:S(2)}) collective-permute-start(f32[1,64,128]{2,1,0:T(8,128)S(1)} %get-tuple-element.264), channel_id=1, source_target_pairs={{1,0},{2,1},{3,2},{5,4},{6,5},{7,6},{9,8},{10,9},{11,10},{13,12},{... | collective-permute-start | bytes 98312 | tf_op jit(solution)/shard_map/ppermute | solution.py:21
  12.5 1.3 collective-permute-start.3
  13.8 5.8 %collective-permute-start.2 = (bf16[2,1,64,128]{3,2,0,1:T(8,128)(2,1)S(1)}, bf16[2,1,64,128]{3,2,0,1:T(8,128)(2,1)S(1)}, u32[]{:S(2)}, u32[]{:S(2)}) collective-permute-start(bf16[2,1,64,128]{3,2,0,1:T(8,128)(2,1)S(1)} %get-tuple-element.261), channel_id=1, source_target_pairs={{0,1},{1,2},{2,3},{4,5},{5,6},{6,7},{8,9},{9,10},{10,11},{12,13},{... | collective-permute-start | bytes 98312 | tf_op jit(solution)/shard_map/ppermute | solution.py:18
  20.4 1.0 convert_reduce_fusion
  21.6 1.0 fusion.66
  22.6 1.0 multiply_convert_fusion
  23.6 1.0 pad_maximum_fusion.2
  29.8 1.1 fusion.14
  31.1 31.4 %all_gather.16 = f32[8,64,64]{2,1,0:T(8,128)S(1)} all-gather(f32[1,64,64]{2,1,0:T(8,128)S(1)} %copy.15), channel_id=1, replica_groups=mesh['tm'=8,'space'=4] {'tm'}, dimensions={0}, use_global_device_ids=true | all-gather | bytes 147456 | tf_op jit(solution)/shard_map/all_gather | solution.py:28
  65.2 6.6 %all-reduce.3 = (f32[]{:T(128)}, f32[]{:T(128)}) all-reduce(f32[]{:T(128)S(6)} %div.27, f32[]{:T(128)S(6)} %div.26), channel_id=1, replica_groups=mesh['tm'=8,'space'=4] {'space'}, use_global_device_ids=true, to_apply=%region_7.8 | all-reduce | flops 2 | bytes 16 | tf_op jit(solution)/shard_map/psum | solution.py:116
  73.9 21.6 %all-reduce.2 = f32[8]{0:T(128)S(1)} all-reduce(f32[8]{0:T(128)S(1)} %dynamic-update-slice), channel_id=1, replica_groups=mesh['tm'=8,'space'=4] {'tm'}, use_global_device_ids=true, to_apply=%add.2 | all-reduce | flops 8 | bytes 64
  95.5 1.3 %maximum_bitcast_fusion = f32[2,1]{0,1:T(1,128)S(1)} fusion(f32[1]{0:T(128)} %bitcast.35, f32[1]{0:T(128)} %bitcast.34), kind=kLoop, calls=%fused_computation.175 | loop fusion | flops 2 | bytes 16 | tf_op jit(solution)/shard_map/reshape.218
  97.0 10.0 %while.29 = (s32[]{:T(128)}, f32[]{:T(128)}, s32[]{:T(128)}, f32[8]{0:T(128)S(1)}, s32[]{:T(128)}) while((s32[]{:T(128)}, f32[]{:T(128)}, s32[]{:T(128)}, f32[8]{0:T(128)S(1)}, s32[]{:T(128)}) %tuple.71), condition=%wide.region_9.10_spmd, body=%wide.region_8.9_spmd.sunk | while | flops 5 | bytes 107 | solution.py:40
  107.6 12.5 %while.30 = (s32[]{:T(128)}, f32[64,64]{1,0:T(8,128)S(1)}, f32[1,64,1024]{2,1,0:T(8,128)S(1)}, s32[]{:T(128)}, f32[8,64,64]{2,1,0:T(8,128)S(1)}, /*index=5*/f32[8,1,64,1024]{3,2,1,0:T(8,128)}, s32[]{:T(128)}, s32[]{:T(128)}) while((s32[]{:T(128)}, f32[64,64]{1,0:T(8,128)S(1)}, f32[1,64,1024]{2,1,0:T(8,128)S(1)}, s32[]{:T(128)}, ...), condition=%wide.region_3.4_spmd.clone, body=%wide.region_2.3_spmd.clone.sunk | while | flops 53743620 | bytes 1755756 | solution.py:40
  107.6 1.3 %fusion.127 = f32[1,64,1024]{2,1,0:T(8,128)S(1)} fusion(f32[1,64,1024]{2,1,0:T(8,128)S(1)} %copy.57, f32[8,1,64,1024]{3,2,1,0:T(8,128)} %get-tuple-element.350, s32[]{:T(128)} %get-tuple-element.337, pred[]{:T(512)S(6)} %compare.11, pred[]{:T(512)S(6)} %lt.106, f32[8,64,64]{2,1,0:T(8,128)S(1)} %get-tuple-element.349), kind=kOutput, calls=%fused_computation.2.clone.1 | convolution fusion | flops 50593792 | bytes 1083904 | tf_op jit(solution)/shard_map/while/body/eval_jaxpr/ij,bjn->bin/dot_general | solution.py:62
  109.2 1.3 %fusion.127 = f32[1,64,1024]{2,1,0:T(8,128)S(1)} fusion(f32[1,64,1024]{2,1,0:T(8,128)S(1)} %copy.57, f32[8,1,64,1024]{3,2,1,0:T(8,128)} %get-tuple-element.350, s32[]{:T(128)} %get-tuple-element.337, pred[]{:T(512)S(6)} %compare.11, pred[]{:T(512)S(6)} %lt.106, f32[8,64,64]{2,1,0:T(8,128)S(1)} %get-tuple-element.349), kind=kOutput, calls=%fused_computation.2.clone.1 | convolution fusion | flops 50593792 | bytes 1083904 | tf_op jit(solution)/shard_map/while/body/eval_jaxpr/ij,bjn->bin/dot_general | solution.py:62
  110.7 1.3 %fusion.127 = f32[1,64,1024]{2,1,0:T(8,128)S(1)} fusion(f32[1,64,1024]{2,1,0:T(8,128)S(1)} %copy.57, f32[8,1,64,1024]{3,2,1,0:T(8,128)} %get-tuple-element.350, s32[]{:T(128)} %get-tuple-element.337, pred[]{:T(512)S(6)} %compare.11, pred[]{:T(512)S(6)} %lt.106, f32[8,64,64]{2,1,0:T(8,128)S(1)} %get-tuple-element.349), kind=kOutput, calls=%fused_computation.2.clone.1 | convolution fusion | flops 50593792 | bytes 1083904 | tf_op jit(solution)/shard_map/while/body/eval_jaxpr/ij,bjn->bin/dot_general | solution.py:62
  112.3 1.3 %fusion.127 = f32[1,64,1024]{2,1,0:T(8,128)S(1)} fusion(f32[1,64,1024]{2,1,0:T(8,128)S(1)} %copy.57, f32[8,1,64,1024]{3,2,1,0:T(8,128)} %get-tuple-element.350, s32[]{:T(128)} %get-tuple-element.337, pred[]{:T(512)S(6)} %compare.11, pred[]{:T(512)S(6)} %lt.106, f32[8,64,64]{2,1,0:T(8,128)S(1)} %get-tuple-element.349), kind=kOutput, calls=%fused_computation.2.clone.1 | convolution fusion | flops 50593792 | bytes 1083904 | tf_op jit(solution)/shard_map/while/body/eval_jaxpr/ij,bjn->bin/dot_general | solution.py:62
  113.9 1.3 %fusion.127 = f32[1,64,1024]{2,1,0:T(8,128)S(1)} fusion(f32[1,64,1024]{2,1,0:T(8,128)S(1)} %copy.57, f32[8,1,64,1024]{3,2,1,0:T(8,128)} %get-tuple-element.350, s32[]{:T(128)} %get-tuple-element.337, pred[]{:T(512)S(6)} %compare.11, pred[]{:T(512)S(6)} %lt.106, f32[8,64,64]{2,1,0:T(8,128)S(1)} %get-tuple-element.349), kind=kOutput, calls=%fused_computation.2.clone.1 | convolution fusion | flops 50593792 | bytes 1083904 | tf_op jit(solution)/shard_map/while/body/eval_jaxpr/ij,bjn->bin/dot_general | solution.py:62
  115.5 1.3 %fusion.127 = f32[1,64,1024]{2,1,0:T(8,128)S(1)} fusion(f32[1,64,1024]{2,1,0:T(8,128)S(1)} %copy.57, f32[8,1,64,1024]{3,2,1,0:T(8,128)} %get-tuple-element.350, s32[]{:T(128)} %get-tuple-element.337, pred[]{:T(512)S(6)} %compare.11, pred[]{:T(512)S(6)} %lt.106, f32[8,64,64]{2,1,0:T(8,128)S(1)} %get-tuple-element.349), kind=kOutput, calls=%fused_computation.2.clone.1 | convolution fusion | flops 50593792 | bytes 1083904 | tf_op jit(solution)/shard_map/while/body/eval_jaxpr/ij,bjn->bin/dot_general | solution.py:62
  117.0 1.3 %fusion.127 = f32[1,64,1024]{2,1,0:T(8,128)S(1)} fusion(f32[1,64,1024]{2,1,0:T(8,128)S(1)} %copy.57, f32[8,1,64,1024]{3,2,1,0:T(8,128)} %get-tuple-element.350, s32[]{:T(128)} %get-tuple-element.337, pred[]{:T(512)S(6)} %compare.11, pred[]{:T(512)S(6)} %lt.106, f32[8,64,64]{2,1,0:T(8,128)S(1)} %get-tuple-element.349), kind=kOutput, calls=%fused_computation.2.clone.1 | convolution fusion | flops 50593792 | bytes 1083904 | tf_op jit(solution)/shard_map/while/body/eval_jaxpr/ij,bjn->bin/dot_general | solution.py:62
  118.6 1.3 %fusion.127 = f32[1,64,1024]{2,1,0:T(8,128)S(1)} fusion(f32[1,64,1024]{2,1,0:T(8,128)S(1)} %copy.57, f32[8,1,64,1024]{3,2,1,0:T(8,128)} %get-tuple-element.350, s32[]{:T(128)} %get-tuple-element.337, pred[]{:T(512)S(6)} %compare.11, pred[]{:T(512)S(6)} %lt.106, f32[8,64,64]{2,1,0:T(8,128)S(1)} %get-tuple-element.349), kind=kOutput, calls=%fused_computation.2.clone.1 | convolution fusion | flops 50593792 | bytes 1083904 | tf_op jit(solution)/shard_map/while/body/eval_jaxpr/ij,bjn->bin/dot_general | solution.py:62
  120.1 1.1 fusion.16
  (94 shorter events, 16.8 us)
Async XLA Ops:
  7.2 100.4 %all-gather.3.cloned.1.call-start = ((), (), s32[]{:S(2)}) async-start(), calls=%async_computation | async-start | bytes 2359296 | tf_op jit(solution)/shard_map/all_gather | solution.py:28
  8.0 13.6 %collective-permute-start = (f32[1,64,128]{2,1,0:T(8,128)S(1)}, f32[1,64,128]{2,1,0:T(8,128)S(1)}, u32[]{:S(2)}, u32[]{:S(2)}) collective-permute-start(f32[1,64,128]{2,1,0:T(8,128)S(1)} %get-tuple-element.263), channel_id=1, source_target_pairs={{0,1},{1,2},{2,3},{4,5},{5,6},{6,7},{8,9},{9,10},{10,11},{12,13},{... | collective-permute-start | bytes 98312 | tf_op jit(solution)/shard_map/ppermute | solution.py:18
  10.4 11.2 %collective-permute-start.1 = (f32[1,64,128]{2,1,0:T(8,128)S(1)}, f32[1,64,128]{2,1,0:T(8,128)S(1)}, u32[]{:S(2)}, u32[]{:S(2)}) collective-permute-start(f32[1,64,128]{2,1,0:T(8,128)S(1)} %get-tuple-element.264), channel_id=1, source_target_pairs={{1,0},{2,1},{3,2},{5,4},{6,5},{7,6},{9,8},{10,9},{11,10},{13,12},{... | collective-permute-start | bytes 98312 | tf_op jit(solution)/shard_map/ppermute | solution.py:21
  12.5 10.1 %collective-permute-start.3 = (bf16[2,1,64,128]{3,2,0,1:T(8,128)(2,1)S(1)}, bf16[2,1,64,128]{3,2,0,1:T(8,128)(2,1)S(1)}, u32[]{:S(2)}, u32[]{:S(2)}) collective-permute-start(bf16[2,1,64,128]{3,2,0,1:T(8,128)(2,1)S(1)} %get-tuple-element.262), channel_id=1, source_target_pairs={{1,0},{2,1},{3,2},{5,4},{6,5},{7,6},{9,8},{10,9},{11,10},{13,12},{... | collective-permute-start | bytes 98312 | tf_op jit(solution)/shard_map/ppermute | solution.py:21
  13.8 8.8 %collective-permute-start.2 = (bf16[2,1,64,128]{3,2,0,1:T(8,128)(2,1)S(1)}, bf16[2,1,64,128]{3,2,0,1:T(8,128)(2,1)S(1)}, u32[]{:S(2)}, u32[]{:S(2)}) collective-permute-start(bf16[2,1,64,128]{3,2,0,1:T(8,128)(2,1)S(1)} %get-tuple-element.261), channel_id=1, source_target_pairs={{0,1},{1,2},{2,3},{4,5},{5,6},{6,7},{8,9},{9,10},{10,11},{12,13},{... | collective-permute-start | bytes 98312 | tf_op jit(solution)/shard_map/ppermute | solution.py:18
  24.9 1.4 %copy-start.2 = (bf16[2,64,576]{2,1,0:T(8,128)(2,1)S(1)}, bf16[2,64,576]{2,1,0:T(8,128)(2,1)}, u32[]{:S(2)}) copy-start(bf16[2,64,576]{2,1,0:T(8,128)(2,1)} %param.9) | copy-start | bytes 442372
  26.1 1.2 copy-start.1
  28.5 1.2 copy-start
  29.0 35.6 %copy-start.3 = (u32[32]{0:T(128)S(1)}, u32[32]{0:T(128)}, u32[]{:S(2)}) copy-start(u32[32]{0:T(128)} %constant.150) | copy-start | bytes 388
Sparse Core Ops, SparseCore 0:
  31.1 51.6 all-gather.2
where the time goes:
time: 129 us; the launch traced here: 128 us
  blocking collectives  59.6 us (46%)
  between operations  17 us (13%)
  matrix products  15.7 us (12%)
  starting transfers between devices  10.8 us (8%)
  other arithmetic  10.3 us (8%)
  local copies, waits for them, and re-layouts  8.86 us (7%)
  loops' own time  5.75 us (4%)
    all_gather x1, blocking collectives, carried_in(): everything = jax.tree.map(lambda part: lax.all_gather(part, axis), shard)  31.4 us
    unnamed x1, blocking collectives  21.6 us
    dot_general x10, matrix products, mix_channels(): return jnp.einsum('ij,bjn->bin', matrix, field, precision=highest)  12.8 us
    ppermute x2, starting transfers between devices, extended(): lax.ppermute(lax.slice_in_dim(block, block.shape[dim] - width, None, axis...  8.17 us
    psum x1, blocking collectives, body(): partial_value = lax.psum(partial_value, 'space')  6.6 us
    another operation x2, loops' own time, carried_in(): return lax.fori_loop(0, peers, turn, start)  5.75 us
    dynamic_slice x8, local copies, waits for them, and re-layouts, turn(): new = combine(before, jax.tree.map(lambda part: part[k], everything))  4.69 us
    another operation x5, other arithmetic  2.76 us
  transfers between devices with their start and end apart: 5, of which 0 were waited for; matrix products, arithmetic and copies ran while one was open for 10% of the time, Pallas kernels for 0%

commit v1 on v0

v1 whole, which is shorter than its diff:
```python
import functools

import jax
import jax.numpy as jnp
from jax import lax
from jax.experimental import pallas as pl
from jax.experimental.pallas import tpu as pltpu
from jax.sharding import PartitionSpec as P

WIDTH = 64
LANES = 128
MESH = pl.DeviceIdType.MESH
step_size = 0.0078125
f32 = jnp.float32
bf16 = jnp.bfloat16


def split(value):
    high = value.astype(bf16)
    low = (value - high.astype(f32)).astype(bf16)
    return high, low


def exact_left(matrix):
    high, low = split(matrix)
    return jnp.concatenate([high.astype(f32), high.astype(f32), low.astype(f32)], axis=1).astype(bf16)


def exact_dot(left, field):
    high, low = split(field)
    return jnp.dot(left, jnp.concatenate([high, low, high], axis=0), preferred_element_type=f32)


def write_taps(target, base, first, count, value, column, row_len):
    width = value.shape[1]
    left = jnp.where(column != 0, pltpu.roll(value, 1, 1), 0.0)
    right = jnp.where(column != row_len - 1, pltpu.roll(value, width - 1, 1), 0.0)
    channels = value.shape[0]
    for dy in (-1, 0, 1):
        for index, source in enumerate((left, value, right)):
            tap = (dy + 1) * 3 + index
            moved = source if dy == 0 else pltpu.roll(source, (-dy * row_len) % width, 1)
            target[tap * channels:(tap + 1) * channels, base:base + count] = moved[:, first:first + count].astype(bf16)


def kernel(peers, strips, guess, kernels, biases, probes, states, logs,
           halo, probe_halo, stack, probe_stack, turned, mine, theirs, own_out, their_off,
           chain_in, chain_out, pass_out, trace_out, trace_in, pair_out, pair_in, run_out, run_in,
           halo_send, halo_recv, mat_sem, off_send, off_recv, chain_send, chain_recv,
           pass_send, pass_recv, trace_send, trace_recv, small_sem):
    row_len = WIDTH
    channels, cells = guess.shape[2], guess.shape[3]
    layers = kernels.shape[0]
    probe_count = probes.shape[0]
    taps = 9
    edge = layers * row_len
    wide = cells + 2 * edge
    rows = cells // row_len
    half = cells // 2
    chunks = half // LANES
    k = lax.axis_index("tm")
    s = lax.axis_index("space")
    q, x = k // 2, k % 2
    partner = q * 2 + 1 - x
    pairs = peers // 2

    def remote(src, dst, send, recv, tm, space):
        return pltpu.make_async_remote_copy(
            src_ref=src, dst_ref=dst, send_sem=send, recv_sem=recv, device_id=(tm, space), device_id_type=MESH)

    def chunk(side, c):
        return pl.ds(pl.multiple_of(side * half + c * LANES, LANES), LANES)

    barrier = pltpu.get_barrier_semaphore()
    for d in range(1, strips):
        pl.semaphore_signal(barrier, inc=1, device_id=(k, lax.rem(s + d, strips)), device_id_type=MESH)
    pl.semaphore_signal(barrier, inc=1, device_id=(partner, s), device_id_type=MESH)

    @pl.when(q > 0)
    def _():
        pl.semaphore_signal(barrier, inc=1, device_id=(k - 2, s), device_id_type=MESH)

    @pl.when(q < pairs - 1)
    def _():
        pl.semaphore_signal(barrier, inc=1, device_id=(k + 2, s), device_id_type=MESH)

    pl.semaphore_wait(barrier, strips + (q > 0).astype(jnp.int32) + (q < pairs - 1).astype(jnp.int32))

    up = remote(guess.at[0, 0, :, pl.ds(cells - edge, edge)], halo.at[0], halo_send.at[0], halo_recv.at[0], k, s + 1)
    down = remote(guess.at[0, 0, :, pl.ds(0, edge)], halo.at[1], halo_send.at[1], halo_recv.at[1], k, s - 1)
    probe_up = remote(probes.at[:, 0, :, pl.ds(cells - edge, edge)], probe_halo.at[0], halo_send.at[2], halo_recv.at[2], k, s + 1)
    probe_down = remote(probes.at[:, 0, :, pl.ds(0, edge)], probe_halo.at[1], halo_send.at[3], halo_recv.at[3], k, s - 1)
    has_up, has_down = s < strips - 1, s > 0

    @pl.when(has_up)
    def _():
        up.start()

    @pl.when(has_down)
    def _():
        down.start()

    @pl.when(has_up)
    def _():
        probe_up.start()

    @pl.when(has_down)
    def _():
        probe_down.start()

    first_pair = jnp.logical_and(q == 0, x == 0)
    seeds = [remote(guess.at[0, 0, :, pl.ds(half + c * LANES, LANES)], chain_in.at[c], pass_send.at[chunks + c], chain_recv.at[c], partner, s)
             for c in range(chunks)]

    @pl.when(first_pair)
    def _():
        for c in range(chunks):
            seeds[c].start()
        for c in range(chunks):
            chain_in[c] = guess[0, 0, :, c * LANES:(c + 1) * LANES]

    total = kernels[0].astype(f32)
    for n in range(1, layers):
        total = total + kernels[n].astype(f32)
    summed = total[:, 0:channels]
    for t in range(1, taps):
        summed = summed + total[:, t * channels:(t + 1) * channels]
    own_matrix = step_size * summed
    mine[:, 0:channels] = own_matrix
    mine[:, channels:2 * channels] = own_matrix
    mat = remote(mine, theirs, mat_sem.at[0], mat_sem.at[1], partner, s)
    mat.start()

    for n in range(layers):
        flipped = kernels[n].astype(f32)
        for t in range(taps):
            block = flipped[:, t * channels:(t + 1) * channels].T
            turned[n * channels:(n + 1) * channels, (taps - 1 - t) * channels:(taps - t) * channels] = block.astype(bf16)

    value = guess[0, 0]
    own_left = exact_left(own_matrix)
    mixed = exact_dot(own_left, value)

    position = lax.broadcasted_iota(jnp.int32, (1, wide), 1)
    column = position % row_len
    row = position // row_len - layers + s * rows
    inside = jnp.logical_and(row >= 0, row < rows * strips)
    diagonal = lax.broadcasted_iota(jnp.int32, (channels, channels), 0) == lax.broadcasted_iota(jnp.int32, (channels, channels), 1)

    @pl.when(has_down)
    def _():
        up.wait_recv()

    @pl.when(has_up)
    def _():
        down.wait_recv()

    current = jnp.concatenate([halo[0], value, halo[1]], axis=1)
    slopes = []
    for n in range(layers):
        activation = jnp.where(inside, jnp.tanh(current), 0.0)
        own = activation[:, edge:edge + cells]
        slopes.append(1.0 - own * own)
        last = n == layers - 1
        first, count = (edge, cells) if last else (0, wide)
        write_taps(stack, first, first, count, activation, column, row_len)
        forcing = jnp.dot(kernels[n], stack[:, first:first + count], preferred_element_type=f32)
        bias = jnp.sum(jnp.where(diagonal, biases[n:n + 1, :], 0.0), axis=1, keepdims=True)
        current = current[:, first:first + count] + step_size * (forcing + bias)
    own_out[...] = (current - value) - mixed

    offs = [remote(own_out.at[:, chunk(1 - x, c)], their_off.at[c], off_send.at[c], off_recv.at[c], partner, s)
            for c in range(chunks)]
    for c in range(chunks):
        offs[c].start()

    @pl.when(has_down)
    def _():
        probe_up.wait_recv()

    @pl.when(has_up)
    def _():
        probe_down.wait_recv()

    sums = [jnp.zeros((8, LANES), f32) for _ in range(layers)]
    for p in range(probe_count):
        field = probes[p, 0].astype(f32)
        padded = jnp.concatenate([probe_halo[0, p].astype(f32), field, probe_halo[1, p].astype(f32)], axis=1)
        padded = jnp.where(inside, padded, 0.0)
        write_taps(probe_stack, 0, edge, cells, padded, column, row_len)
        weights = jnp.dot(turned[...], probe_stack[...], preferred_element_type=f32)
        for n in range(layers):
            tangent = (slopes[n] * field).astype(bf16).astype(f32)
            product = tangent * weights[n * channels:(n + 1) * channels]
            part = product[:, 0:LANES]
            for c in range(1, cells // LANES):
                part = part + product[:, c * LANES:(c + 1) * LANES]
            for r in range(channels // 8):
                sums[n] = sums[n] + part[r * 8:(r + 1) * 8]
    for n in range(layers):
        trace_out[n * 8:(n + 1) * 8] = sums[n]
    traces = [remote(trace_out, trace_in.at[d - 1], trace_send.at[d - 1], trace_recv.at[d - 1], k, lax.rem(s + d, strips))
              for d in range(1, strips)]
    for copy in traces:
        copy.start()

    mat.wait_recv()
    other_matrix = theirs[:, 0:channels]
    even = x == 0
    early = jnp.where(even, own_matrix, other_matrix)
    late = jnp.where(even, other_matrix, own_matrix)
    late_left = exact_left(late)
    both = early + late + exact_dot(late_left, early)
    map_left = exact_left(jnp.concatenate([both, early], axis=0))

    nexts = [remote(chain_out.at[c], chain_in.at[c], chain_send.at[c], chain_recv.at[c], k + 2, s) for c in range(chunks)]
    passes = [remote(pass_out.at[c], states.at[0, 0, :, chunk(x, c)], pass_send.at[c], pass_recv.at[c], partner, s)
              for c in range(chunks)]
    passed = [remote(pass_out.at[c], states.at[0, 0, :, chunk(1 - x, c)], pass_send.at[c], pass_recv.at[c], partner, s)
              for c in range(chunks)]
    pair = remote(pair_out, pair_in, small_sem.at[0], small_sem.at[1], partner, s)
    onward = remote(run_out, run_in, small_sem.at[2], small_sem.at[3], k + 2, s)
    go_on = q < pairs - 1
    waits = jnp.logical_not(first_pair)
    early_offs, sum_offs = [], []
    for c in range(chunks):
        offs[c].wait_recv()
        held = own_out[:, chunk(x, c)]
        got = their_off[c]
        early_off = jnp.where(even, held, got)
        late_off = jnp.where(even, got, held)
        early_offs.append(early_off)
        sum_offs.append(late_off + early_off + exact_dot(late_left, early_off))
    for c in range(chunks):
        @pl.when(waits)
        def _():
            nexts[c].wait_recv()

        here = chain_in[c]
        moved = exact_dot(map_left, here)
        chain_out[c] = here + (moved[0:channels] + sum_offs[c])

        @pl.when(go_on)
        def _():
            nexts[c].start()

        between = here + (moved[channels:2 * channels] + early_offs[c])
        pass_out[c] = jnp.where(even, between, here)
        passes[c].start()
        states[0, 0, :, chunk(x, c)] = jnp.where(even, here, between)
        if c == max(chunks - 2, 0):
            trace_total = trace_out[...]
            for copy in traces:
                copy.wait_recv()
            for d in range(1, strips):
                trace_total = trace_total + trace_in[d - 1]
            pair_out[...] = trace_total
            pair.start()

    pair.wait_recv()

    def layer_sum(tile):
        result = tile[0:8]
        for n in range(1, layers):
            result = result + tile[n * 8:(n + 1) * 8]
        return result

    own_sum, pair_sum = layer_sum(trace_total), layer_sum(pair_in[...])

    @pl.when(q == 0)
    def _():
        run_in[...] = jnp.zeros_like(run_in)

    @pl.when(q > 0)
    def _():
        onward.wait_recv()

    running = run_in[...]
    run_out[...] = running + own_sum + pair_sum

    @pl.when(go_on)
    def _():
        onward.start()

    running = running + jnp.where(even, 0.0, pair_sum)
    for n in range(layers):
        running = running + trace_total[n * 8:(n + 1) * 8]
        logs[n] = jnp.sum(running) * (-(step_size / row_len) / probe_count)

    for c in range(chunks):
        passed[c].wait_recv()
    for c in range(chunks):
        passes[c].wait_send()
        offs[c].wait_send()
    for copy in traces:
        copy.wait_send()
    mat.wait_send()
    pair.wait_send()

    @pl.when(go_on)
    def _():
        for c in range(chunks):
            nexts[c].wait_send()
        onward.wait_send()

    @pl.when(first_pair)
    def _():
        for c in range(chunks):
            seeds[c].wait_send()

    @pl.when(has_up)
    def _():
        up.wait_send()
        probe_up.wait_send()

    @pl.when(has_down)
    def _():
        down.wait_send()
        probe_down.wait_send()


def solution(mesh):
    peers, strips = mesh.shape["tm"], mesh.shape["space"]

    def step(guess, kernels, biases, probes):
        channels, cells = guess.shape[2], guess.shape[3]
        layers = kernels.shape[0]
        probe_count = probes.shape[0]
        edge = layers * WIDTH
        chunks = cells // 2 // LANES
        depth = kernels.shape[2]
        dma = pltpu.SemaphoreType.DMA
        tile = (chunks, channels, LANES)
        return pl.pallas_call(
            functools.partial(kernel, peers, strips),
            out_shape=(
                jax.ShapeDtypeStruct(guess.shape, f32),
                jax.ShapeDtypeStruct((layers,), f32),
            ),
            in_specs=[pl.BlockSpec(memory_space=pltpu.VMEM)] * 4,
            out_specs=(pl.BlockSpec(memory_space=pltpu.VMEM), pl.BlockSpec(memory_space=pltpu.SMEM)),
            scratch_shapes=[
                pltpu.VMEM((2, channels, edge), f32),
                pltpu.VMEM((2, probe_count, channels, edge), bf16),
                pltpu.VMEM((depth, cells + 2 * edge), bf16),
                pltpu.VMEM((depth, cells), bf16),
                pltpu.VMEM((layers * channels, depth), bf16),
                pltpu.VMEM((channels, 2 * channels), f32),
                pltpu.VMEM((channels, 2 * channels), f32),
                pltpu.VMEM((channels, cells), f32),
                pltpu.VMEM(tile, f32),
                pltpu.VMEM(tile, f32),
                pltpu.VMEM(tile, f32),
                pltpu.VMEM(tile, f32),
                pltpu.VMEM((layers * 8, LANES), f32),
                pltpu.VMEM((max(strips - 1, 1), layers * 8, LANES), f32),
                pltpu.VMEM((layers * 8, LANES), f32),
                pltpu.VMEM((layers * 8, LANES), f32),
                pltpu.VMEM((8, LANES), f32),
                pltpu.VMEM((8, LANES), f32),
                dma((4,)), dma((4,)), dma((2,)), dma((chunks,)), dma((chunks,)), dma((chunks,)), dma((chunks,)),
                dma((2 * chunks,)), dma((chunks,)), dma((max(strips - 1, 1),)), dma((max(strips - 1, 1),)), dma((4,)),
            ],
            compiler_params=pltpu.CompilerParams(collective_id=0, has_side_effects=True),
        )(guess, kernels, biases, probes)

    return jax.shard_map(
        step,
        mesh=mesh,
        in_specs=(
            P("tm", None, None, "space"),
            P("tm", None, None),
            P("tm", None),
            P(None, None, None, "space"),
        ),
        out_specs=(P("tm", None, None, "space"), P("tm")),
        check_vma=False,
    )
```

time: 129 us -> 27 us (0.21)
  the two profiles are of different devices: /device:TPU:0 before, /device:TPU:24 now
where the time goes in v1:
time: 27 us; the launch traced here: 26.8 us
  Pallas kernels  24 us (89%)
  local copies, waits for them, and re-layouts  2.19 us (8%)
  between operations  0.65 us (2%)
    pallas_call x1, Pallas kernels, step(): pl.pallas_call(functools.partial(kernel, peers, strips), out_shape=(jax.S...  24 us
    unnamed x4, local copies, waits for them, and re-layouts  2.19 us

profile of v1, /device:TPU:24, one launch (start us, length us, event | category | flops | bytes accessed | tf_op | source)
XLA Modules:
  0.0 26.8 jit_solution(17355173799842075592)
XLA Ops:
  0.6 24.0 %shard_map.59 = (f32[1,1,64,1024]{3,2,1,0:T(8,128)}, f32[2]{0:T(128)}) custom-call(f32[1,1,64,1024]{3,2,1,0:T(8,128)} %guess.1, bf16[2,64,576]{2,1,0:T(8,128)(2,1)} %kernels.1, f32[2,64]{1,0:T(2,128)} %biases.1, bf16[2,1,64,1024]{3,2,1,0:T(8,128)(2,1)} %probes.1), custom_call_target="tpu_custom_call" | custom-call | tf_op jit(solution)/shard_map/pallas_call | solution.py:334
  24.7 0.0 copy-start
  24.7 1.7 %copy.8 = f32[1,1,64,1024]{3,2,1,0:T(8,128)} copy(f32[1,1,64,1024]{3,2,1,0:T(8,128)} %get-tuple-element.4) | data formatting | bytes 524288
  26.3 0.0 copy-done
  26.3 0.5 %copy.9 = f32[2]{0:T(128)} copy(f32[2]{0:T(128)S(1)} %copy-done) | data formatting | bytes 16
Async XLA Ops:
  24.7 1.7 %copy-start = (f32[2]{0:T(128)S(1)}, f32[2]{0:T(128)}, u32[]{:S(2)}) copy-start(f32[2]{0:T(128)} %get-tuple-element.5) | copy-start | bytes 28

commit v2 on v1

--- a/solution.py
+++ b/solution.py
@@ -43,8 +43,8 @@
             target[tap * channels:(tap + 1) * channels, base:base + count] = moved[:, first:first + count].astype(bf16)
 
 
-def kernel(peers, strips, guess, kernels, biases, probes, states, logs,
-           halo, probe_halo, stack, probe_stack, turned, mine, theirs, own_out, their_off,
+def kernel(peers, strips, guess_in, kernels_in, biases_in, probes_in, states, logs,
+           guess, kernels, biases, probes, load_sem, halo, probe_halo, stack, probe_stack, turned, mine, theirs, own_out, their_off,
            chain_in, chain_out, pass_out, trace_out, trace_in, pair_out, pair_in, run_out, run_in,
            halo_send, halo_recv, mat_sem, off_send, off_recv, chain_send, chain_recv,
            pass_send, pass_recv, trace_send, trace_recv, small_sem):
@@ -71,6 +71,11 @@
     def chunk(side, c):
         return pl.ds(pl.multiple_of(side * half + c * LANES, LANES), LANES)
 
+    loads = [pltpu.make_async_copy(src, dst, load_sem.at[i]) for i, (src, dst) in enumerate(
+        ((kernels_in, kernels), (guess_in, guess), (biases_in, biases), (probes_in, probes)))]
+    for load in loads:
+        load.start()
+
     barrier = pltpu.get_barrier_semaphore()
     for d in range(1, strips):
         pl.semaphore_signal(barrier, inc=1, device_id=(k, lax.rem(s + d, strips)), device_id_type=MESH)
@@ -86,10 +91,10 @@
 
     pl.semaphore_wait(barrier, strips + (q > 0).astype(jnp.int32) + (q < pairs - 1).astype(jnp.int32))
 
-    up = remote(guess.at[0, 0, :, pl.ds(cells - edge, edge)], halo.at[0], halo_send.at[0], halo_recv.at[0], k, s + 1)
-    down = remote(guess.at[0, 0, :, pl.ds(0, edge)], halo.at[1], halo_send.at[1], halo_recv.at[1], k, s - 1)
-    probe_up = remote(probes.at[:, 0, :, pl.ds(cells - edge, edge)], probe_halo.at[0], halo_send.at[2], halo_recv.at[2], k, s + 1)
-    probe_down = remote(probes.at[:, 0, :, pl.ds(0, edge)], probe_halo.at[1], halo_send.at[3], halo_recv.at[3], k, s - 1)
+    up = remote(guess_in.at[0, 0, :, pl.ds(cells - edge, edge)], halo.at[0], halo_send.at[0], halo_recv.at[0], k, s + 1)
+    down = remote(guess_in.at[0, 0, :, pl.ds(0, edge)], halo.at[1], halo_send.at[1], halo_recv.at[1], k, s - 1)
+    probe_up = remote(probes_in.at[:, 0, :, pl.ds(cells - edge, edge)], probe_halo.at[0], halo_send.at[2], halo_recv.at[2], k, s + 1)
+    probe_down = remote(probes_in.at[:, 0, :, pl.ds(0, edge)], probe_halo.at[1], halo_send.at[3], halo_recv.at[3], k, s - 1)
     has_up, has_down = s < strips - 1, s > 0
 
     @pl.when(has_up)
@@ -109,13 +114,19 @@
         probe_down.start()
 
     first_pair = jnp.logical_and(q == 0, x == 0)
-    seeds = [remote(guess.at[0, 0, :, pl.ds(half + c * LANES, LANES)], chain_in.at[c], pass_send.at[chunks + c], chain_recv.at[c], partner, s)
+    seeds = [remote(guess_in.at[0, 0, :, pl.ds(half + c * LANES, LANES)], chain_in.at[c], pass_send.at[chunks + c], chain_recv.at[c], partner, s)
              for c in range(chunks)]
 
     @pl.when(first_pair)
     def _():
         for c in range(chunks):
             seeds[c].start()
+
+    for load in loads:
+        load.wait()
+
+    @pl.when(first_pair)
+    def _():
         for c in range(chunks):
             chain_in[c] = guess[0, 0, :, c * LANES:(c + 1) * LANES]
 
@@ -222,29 +233,27 @@
     onward = remote(run_out, run_in, small_sem.at[2], small_sem.at[3], k + 2, s)
     go_on = q < pairs - 1
     waits = jnp.logical_not(first_pair)
-    early_offs, sum_offs = [], []
     for c in range(chunks):
         offs[c].wait_recv()
         held = own_out[:, chunk(x, c)]
         got = their_off[c]
         early_off = jnp.where(even, held, got)
         late_off = jnp.where(even, got, held)
-        early_offs.append(early_off)
-        sum_offs.append(late_off + early_off + exact_dot(late_left, early_off))
-    for c in range(chunks):
+        sum_off = late_off + early_off + exact_dot(late_left, early_off)
+
         @pl.when(waits)
         def _():
             nexts[c].wait_recv()
 
         here = chain_in[c]
         moved = exact_dot(map_left, here)
-        chain_out[c] = here + (moved[0:channels] + sum_offs[c])
+        chain_out[c] = here + (moved[0:channels] + sum_off)
 
         @pl.when(go_on)
         def _():
             nexts[c].start()
 
-        between = here + (moved[channels:2 * channels] + early_offs[c])
+        between = here + (moved[channels:2 * channels] + early_off)
         pass_out[c] = jnp.where(even, between, here)
         passes[c].start()
         states[0, 0, :, chunk(x, c)] = jnp.where(even, here, between)
@@ -285,7 +294,7 @@
     running = running + jnp.where(even, 0.0, pair_sum)
     for n in range(layers):
         running = running + trace_total[n * 8:(n + 1) * 8]
-        logs[n] = jnp.sum(running) * (-(step_size / row_len) / probe_count)
+        logs[n * 8:(n + 1) * 8] = running * (-(step_size / row_len) / probe_count)
 
     for c in range(chunks):
         passed[c].wait_recv()
@@ -319,6 +328,14 @@
         probe_down.wait_send()
 
 
+def finish(states_in, tiles, states, logs, sem):
+    copy = pltpu.make_async_copy(states_in, states, sem)
+    copy.start()
+    for n in range(logs.shape[0]):
+        logs[n] = jnp.sum(tiles[n * 8:(n + 1) * 8])
+    copy.wait()
+
+
 def solution(mesh):
     peers, strips = mesh.shape["tm"], mesh.shape["space"]
 
@@ -331,15 +348,20 @@
         depth = kernels.shape[2]
         dma = pltpu.SemaphoreType.DMA
         tile = (chunks, channels, LANES)
-        return pl.pallas_call(
+        states, tiles = pl.pallas_call(
             functools.partial(kernel, peers, strips),
             out_shape=(
-                jax.ShapeDtypeStruct(guess.shape, f32),
-                jax.ShapeDtypeStruct((layers,), f32),
+                pltpu.VMEM(guess.shape, f32),
+                pltpu.VMEM((layers * 8, LANES), f32),
             ),
-            in_specs=[pl.BlockSpec(memory_space=pltpu.VMEM)] * 4,
-            out_specs=(pl.BlockSpec(memory_space=pltpu.VMEM), pl.BlockSpec(memory_space=pltpu.SMEM)),
+            in_specs=[pl.BlockSpec(memory_space=pl.ANY)] * 4,
+            out_specs=(pl.BlockSpec(memory_space=pltpu.VMEM), pl.BlockSpec(memory_space=pltpu.VMEM)),
             scratch_shapes=[
+                pltpu.VMEM(guess.shape, guess.dtype),
+                pltpu.VMEM(kernels.shape, kernels.dtype),
+                pltpu.VMEM(biases.shape, biases.dtype),
+                pltpu.VMEM(probes.shape, probes.dtype),
+                dma((4,)),
                 pltpu.VMEM((2, channels, edge), f32),
                 pltpu.VMEM((2, probe_count, channels, edge), bf16),
                 pltpu.VMEM((depth, cells + 2 * edge), bf16),
@@ -363,6 +385,16 @@
             ],
             compiler_params=pltpu.CompilerParams(collective_id=0, has_side_effects=True),
         )(guess, kernels, biases, probes)
+        return pl.pallas_call(
+            finish,
+            out_shape=(
+                jax.ShapeDtypeStruct(guess.shape, f32),
+                jax.ShapeDtypeStruct((layers,), f32),
+            ),
+            in_specs=[pl.BlockSpec(memory_space=pltpu.VMEM)] * 2,
+            out_specs=(pl.BlockSpec(memory_space=pl.ANY), pl.BlockSpec(memory_space=pltpu.SMEM)),
+            scratch_shapes=[dma],
+        )(pltpu.with_memory_space_constraint(states, pltpu.VMEM), pltpu.with_memory_space_constraint(tiles, pltpu.VMEM))
 
     return jax.shard_map(
         step,

time: 27 us -> 23.5 us (0.87)
  local copies, waits for them, and re-layouts: 2.19 us -> 0 us
  Pallas kernels: 24 us -> 22.7 us
    unnamed x4 -> x0, local copies, waits for them, and re-layouts: 2.19 us -> none
    pallas_call x1 -> x2, Pallas kernels: 24 us -> 22.7 us  [the longest x1 21.5 us: step(): pl.pallas_call(functools.partial(kernel, peers, strips), out_shape=(pltpu...]
where the time goes in v2:
time: 23.5 us; the launch traced here: 23.3 us
  Pallas kernels  22.7 us (97%)
  between operations  0.64 us (3%)
    pallas_call x1, Pallas kernels, step(): pl.pallas_call(functools.partial(kernel, peers, strips), out_shape=(pltpu...  21.5 us
    pallas_call x1, Pallas kernels, step(): pl.pallas_call(finish, out_shape=(jax.ShapeDtypeStruct(guess.shape, f32),...  1.23 us

profile of v2, /device:TPU:24, one launch (start us, length us, event | category | flops | bytes accessed | tf_op | source)
XLA Modules:
  0.0 23.3 jit_solution(3002356580908775061)
XLA Ops:
  0.6 21.5 %shard_map.59 = (f32[1,1,64,1024]{3,2,1,0:T(8,128)S(1)}, f32[16,128]{1,0:T(8,128)S(1)}) custom-call(f32[1,1,64,1024]{3,2,1,0:T(8,128)} %guess_in.1, bf16[2,64,576]{2,1,0:T(8,128)(2,1)} %kernels_in.1, f32[2,64]{1,0:T(2,128)} %biases_in.1, bf16[2,1,64,1024]{3,2,1,0:T(8,128)(2,1)} %probes_in.1), custom_call_target="tpu_custom_call" | custom-call | tf_op jit(solution)/shard_map/pallas_call | solution.py:351
  22.1 1.2 %shard_map.60 = (f32[1,1,64,1024]{3,2,1,0:T(8,128)}, f32[2]{0:T(128)}) custom-call(f32[1,1,64,1024]{3,2,1,0:T(8,128)S(1)} %get-tuple-element.4.states_in, f32[16,128]{1,0:T(8,128)S(1)} %get-tuple-element.5.tiles), custom_call_target="tpu_custom_call" | custom-call | tf_op jit(solution)/shard_map/pallas_call | solution.py:388

commit v3 on v2

v3 whole, which is shorter than its diff:
```python
import functools

import jax
import jax.numpy as jnp
from jax import lax
from jax.experimental import pallas as pl
from jax.experimental.pallas import tpu as pltpu
from jax.sharding import PartitionSpec as P

WIDTH = 64
LANES = 128
MESH = pl.DeviceIdType.MESH
step_size = 0.0078125
f32 = jnp.float32
bf16 = jnp.bfloat16


def split(value):
    high = value.astype(bf16)
    low = (value - high.astype(f32)).astype(bf16)
    return high, low


def exact_left(matrix):
    high, low = split(matrix)
    return jnp.concatenate([high.astype(f32), high.astype(f32), low.astype(f32)], axis=1).astype(bf16)


def exact_dot(left, field):
    high, low = split(field)
    return jnp.dot(left, jnp.concatenate([high, low, high], axis=0), preferred_element_type=f32)


def write_taps(target, base, first, count, value, column, row_len):
    width = value.shape[1]
    left = jnp.where(column != 0, pltpu.roll(value, 1, 1), 0.0)
    right = jnp.where(column != row_len - 1, pltpu.roll(value, width - 1, 1), 0.0)
    channels = value.shape[0]
    for dy in (-1, 0, 1):
        for index, source in enumerate((left, value, right)):
            tap = (dy + 1) * 3 + index
            moved = source if dy == 0 else pltpu.roll(source, (-dy * row_len) % width, 1)
            target[tap * channels:(tap + 1) * channels, base:base + count] = moved[:, first:first + count].astype(bf16)


def kernel(peers, strips, guess_in, kernels_in, biases_in, probes_in, states, logs,
           window, kernels, biases, probes, stack, probe_stack, turned, offsets, slopes, sum_offs,
           chain_in, chain_out, pass_out, trace_out, trace_in, run_out, run_in,
           load_sem, edge_send, edge_recv, swap_send, swap_recv, chain_send, chain_recv,
           pass_send, pass_recv, trace_send, trace_recv, run_sem):
    row_len = WIDTH
    channels, cells = guess_in.shape[2], guess_in.shape[3]
    layers = kernels_in.shape[0]
    probe_count = probes_in.shape[0]
    taps = 9
    edge = layers * row_len
    rows = cells // row_len
    half = cells // 2
    part = half + edge
    wide = half + 2 * edge
    chunks = half // LANES
    k = lax.axis_index("tm")
    s = lax.axis_index("space")
    q, x = k // 2, k % 2
    other = 1 - x
    partner = q * 2 + other
    pairs = peers // 2
    even = x == 0

    def remote(src, dst, send, recv, tm, space):
        return pltpu.make_async_remote_copy(
            src_ref=src, dst_ref=dst, send_sem=send, recv_sem=recv, device_id=(tm, space), device_id_type=MESH)

    def chunk(side, c):
        return pl.ds(pl.multiple_of(side * half + c * LANES, LANES), LANES)

    def aligned(start, size):
        return pl.ds(pl.multiple_of(start, LANES), size)

    mine = aligned(x * (half - edge), part)
    place = aligned(other * edge, part)
    loads = [pltpu.make_async_copy(src, dst, load_sem.at[i]) for i, (src, dst) in enumerate((
        (guess_in.at[0, 0, :, mine], window.at[x, :, place]),
        (kernels_in, kernels.at[x]),
        (biases_in, biases.at[x]),
        (probes_in.at[:, 0, :, mine], probes.at[:, :, place])))]
    for load in loads:
        load.start()

    barrier = pltpu.get_barrier_semaphore()
    spot = x * strips + s
    ring = []
    for d in range(1, 2 * strips):
        to = lax.rem(spot + d, 2 * strips)
        ring.append((q * 2 + to // strips, lax.rem(to, strips)))
    for tm, space in ring:
        pl.semaphore_signal(barrier, inc=1, device_id=(tm, space), device_id_type=MESH)

    @pl.when(q > 0)
    def _():
        pl.semaphore_signal(barrier, inc=1, device_id=(k - 2, s), device_id_type=MESH)

    @pl.when(q < pairs - 1)
    def _():
        pl.semaphore_signal(barrier, inc=1, device_id=(k + 2, s), device_id_type=MESH)

    pl.semaphore_wait(barrier, 2 * strips - 1 + (q > 0).astype(jnp.int32) + (q < pairs - 1).astype(jnp.int32))

    has_up, has_down = s < strips - 1, s > 0
    last_rows, first_rows = pl.ds(cells - edge, edge), pl.ds(0, edge)
    up = remote(guess_in.at[0, 0, :, last_rows], window.at[x, :, pl.ds(0, edge)], edge_send.at[0], edge_recv.at[x], q * 2, s + 1)
    down = remote(guess_in.at[0, 0, :, first_rows], window.at[x, :, pl.ds(part, edge)], edge_send.at[1], edge_recv.at[x], q * 2 + 1, s - 1)
    probe_up = remote(probes_in.at[:, 0, :, last_rows], probes.at[:, :, pl.ds(0, edge)], edge_send.at[2], edge_recv.at[2], k, s + 1)
    probe_down = remote(probes_in.at[:, 0, :, first_rows], probes.at[:, :, pl.ds(part, edge)], edge_send.at[2], edge_recv.at[2], k, s - 1)
    theirs = aligned(other * (half - edge), part)
    swaps = [
        remote(guess_in.at[0, 0, :, theirs], window.at[x, :, aligned(x * edge, part)], swap_send.at[0], swap_recv.at[0], partner, s),
        remote(kernels_in, kernels.at[x], swap_send.at[1], swap_recv.at[1], partner, s),
        remote(biases_in, biases.at[x], swap_send.at[2], swap_recv.at[2], partner, s),
    ]
    send_probe_up = jnp.logical_and(even, has_up)
    send_probe_down = jnp.logical_and(x == 1, has_down)

    @pl.when(has_up)
    def _():
        up.start()

    @pl.when(has_down)
    def _():
        down.start()

    for i in (1, 0, 2):
        swaps[i].start()

    @pl.when(send_probe_up)
    def _():
        probe_up.start()

    @pl.when(send_probe_down)
    def _():
        probe_down.start()

    def wait_edge(group):
        left = remote(guess_in.at[0, 0, :, last_rows], window.at[group, :, pl.ds(0, edge)], edge_send.at[0], edge_recv.at[group], k, s)
        right = remote(guess_in.at[0, 0, :, first_rows], window.at[group, :, pl.ds(part, edge)], edge_send.at[1], edge_recv.at[group], k, s)

        @pl.when(jnp.logical_and(even, has_down))
        def _():
            left.wait_recv()

        @pl.when(jnp.logical_and(x == 1, has_up))
        def _():
            right.wait_recv()

    position = lax.broadcasted_iota(jnp.int32, (1, wide), 1)
    column = position % row_len
    row = position // row_len - layers + s * rows + x * (rows // 2)
    inside = jnp.logical_and(row >= 0, row < rows * strips)
    diagonal = lax.broadcasted_iota(jnp.int32, (channels, channels), 0) == lax.broadcasted_iota(jnp.int32, (channels, channels), 1)

    def prepare(group):
        total = kernels[group, 0].astype(f32)
        for n in range(1, layers):
            total = total + kernels[group, n].astype(f32)
        summed = total[:, 0:channels]
        for t in range(1, taps):
            summed = summed + total[:, t * channels:(t + 1) * channels]
        return step_size * summed

    def turn(group):
        for n in range(layers):
            flipped = kernels[group, n].astype(f32)
            for t in range(taps):
                block = flipped[:, t * channels:(t + 1) * channels].T
                turned[group, n * channels:(n + 1) * channels, (taps - 1 - t) * channels:(taps - t) * channels] = block.astype(bf16)

    def evolve(group, matrix):
        current = window[group]
        value = current[:, edge:edge + half]
        mixed = exact_dot(exact_left(matrix), value)
        for n in range(layers):
            activation = jnp.where(inside, jnp.tanh(current), 0.0)
            own = activation[:, edge:edge + half]
            slopes[group, n] = 1.0 - own * own
            last = n == layers - 1
            first, count = (edge, half) if last else (0, wide)
            write_taps(stack, first, first, count, activation, column, row_len)
            forcing = jnp.dot(kernels[group, n], stack[:, first:first + count], preferred_element_type=f32)
            bias = jnp.sum(jnp.where(diagonal, biases[group, n:n + 1, :], 0.0), axis=1, keepdims=True)
            current = current[:, first:first + count] + step_size * (forcing + bias)
        offsets[group] = (current - value) - mixed

    for load in loads:
        load.wait()
    own_matrix = prepare(x)
    turn(x)
    wait_edge(x)
    evolve(x, own_matrix)

    arrivals = [
        remote(guess_in.at[0, 0, :, mine], window.at[other, :, place], swap_send.at[0], swap_recv.at[0], partner, s),
        remote(kernels_in, kernels.at[other], swap_send.at[1], swap_recv.at[1], partner, s),
        remote(biases_in, biases.at[other], swap_send.at[2], swap_recv.at[2], partner, s),
    ]
    for arrival in arrivals:
        arrival.wait_recv()
    other_matrix = prepare(other)
    wait_edge(other)
    evolve(other, other_matrix)

    early = jnp.where(even, own_matrix, other_matrix)
    late = jnp.where(even, other_matrix, own_matrix)
    late_left = exact_left(late)
    both = early + late + exact_dot(late_left, early)
    map_left = exact_left(jnp.concatenate([both, early], axis=0))
    early_off = offsets[0]
    sum_offs[...] = offsets[1] + early_off + exact_dot(late_left, early_off)

    trace_copies = [remote(trace_out, trace_in.at[d], trace_send.at[d], trace_recv.at[d], ring[d][0], ring[d][1])
                    for d in range(2 * strips - 1)]

    def strip_traces():
        left = remote(probes_in.at[:, 0, :, last_rows], probes.at[:, :, pl.ds(0, edge)], edge_send.at[2], edge_recv.at[2], k, s)
        right = remote(probes_in.at[:, 0, :, first_rows], probes.at[:, :, pl.ds(part, edge)], edge_send.at[2], edge_recv.at[2], k, s)

        @pl.when(jnp.logical_and(even, has_down))
        def _():
            left.wait_recv()

        @pl.when(jnp.logical_and(x == 1, has_up))
        def _():
            right.wait_recv()

        turn(other)
        sums = [jnp.zeros((8, LANES), f32) for _ in range(2 * layers)]
        for p in range(probe_count):
            padded = jnp.where(inside, probes[p].astype(f32), 0.0)
            field = padded[:, edge:edge + half]
            write_taps(probe_stack, 0, edge, half, padded, column, row_len)
            for group in range(2):
                weights = jnp.dot(turned[group], probe_stack[...], preferred_element_type=f32)
                for n in range(layers):
                    tangent = (slopes[group, n] * field).astype(bf16).astype(f32)
                    product = tangent * weights[n * channels:(n + 1) * channels]
                    folded = product[:, 0:LANES]
                    for c in range(1, chunks):
                        folded = folded + product[:, c * LANES:(c + 1) * LANES]
                    for r in range(channels // 8):
                        sums[group * layers + n] = sums[group * layers + n] + folded[r * 8:(r + 1) * 8]
        for i in range(2 * layers):
            trace_out[i * 8:(i + 1) * 8] = sums[i]
        for copy in trace_copies:
            copy.start()

    @pl.when(q > 0)
    def _():
        strip_traces()

    nexts = [remote(chain_out.at[c], chain_in.at[c], chain_send.at[c], chain_recv.at[c], k + 2, s) for c in range(chunks)]
    passes = [remote(pass_out.at[c], states.at[0, 0, :, chunk(x, c)], pass_send.at[c], pass_recv.at[c], partner, s)
              for c in range(chunks)]
    passed = [remote(pass_out.at[c], states.at[0, 0, :, chunk(1 - x, c)], pass_send.at[c], pass_recv.at[c], partner, s)
              for c in range(chunks)]
    onward = remote(run_out, run_in, run_sem.at[0], run_sem.at[1], k + 2, s)
    go_on = q < pairs - 1

    for c in range(chunks):
        piece = slice(c * LANES, (c + 1) * LANES)

        @pl.when(q == 0)
        def _():
            chain_in[c] = window[0, :, edge + c * LANES:edge + (c + 1) * LANES]

        @pl.when(q > 0)
        def _():
            nexts[c].wait_recv()

        here = chain_in[c]
        moved = exact_dot(map_left, here)
        chain_out[c] = here + (moved[0:channels] + sum_offs[:, piece])

        @pl.when(go_on)
        def _():
            nexts[c].start()

        between = here + (moved[channels:2 * channels] + offsets[0, :, piece])
        pass_out[c] = jnp.where(even, between, here)
        passes[c].start()
        states[0, 0, :, chunk(x, c)] = jnp.where(even, here, between)

    @pl.when(q == 0)
    def _():
        strip_traces()

    for copy in trace_copies:
        copy.wait_recv()
    total = trace_out[...]
    for d in range(2 * strips - 1):
        total = total + trace_in[d]
    group_sums = []
    for group in range(2):
        tile = total[group * layers * 8:(group * layers + 1) * 8]
        for n in range(1, layers):
            tile = tile + total[(group * layers + n) * 8:(group * layers + n + 1) * 8]
        group_sums.append(tile)

    @pl.when(q == 0)
    def _():
        run_in[...] = jnp.zeros_like(run_in)

    @pl.when(q > 0)
    def _():
        onward.wait_recv()

    running = run_in[...]
    run_out[...] = running + group_sums[0] + group_sums[1]

    @pl.when(go_on)
    def _():
        onward.start()

    running = running + jnp.where(even, 0.0, group_sums[0])
    for n in range(layers):
        low, high = n * 8, (layers + n) * 8
        running = running + jnp.where(even, total[low:low + 8], total[high:high + 8])
        logs[n * 8:(n + 1) * 8] = running * (-(step_size / row_len) / probe_count)

    for c in range(chunks):
        passed[c].wait_recv()
    for c in range(chunks):
        passes[c].wait_send()
    for copy in trace_copies:
        copy.wait_send()
    for copy in swaps:
        copy.wait_send()

    @pl.when(go_on)
    def _():
        for c in range(chunks):
            nexts[c].wait_send()
        onward.wait_send()

    @pl.when(has_up)
    def _():
        up.wait_send()

    @pl.when(has_down)
    def _():
        down.wait_send()

    @pl.when(send_probe_up)
    def _():
        probe_up.wait_send()

    @pl.when(send_probe_down)
    def _():
        probe_down.wait_send()


def finish(states_in, tiles, states, logs, sem):
    pieces = sem.shape[0]
    size = states_in.shape[2] // pieces
    copies = [pltpu.make_async_copy(states_in.at[:, :, pl.ds(i * size, size)], states.at[:, :, pl.ds(i * size, size)], sem.at[i])
              for i in range(pieces)]
    for copy in copies:
        copy.start()
    for n in range(logs.shape[0]):
        logs[n] = jnp.sum(tiles[n * 8:(n + 1) * 8])
    for copy in copies:
        copy.wait()


def solution(mesh):
    peers, strips = mesh.shape["tm"], mesh.shape["space"]

    def step(guess, kernels, biases, probes):
        channels, cells = guess.shape[2], guess.shape[3]
        layers = kernels.shape[0]
        probe_count = probes.shape[0]
        edge = layers * WIDTH
        half = cells // 2
        chunks = half // LANES
        depth = kernels.shape[2]
        dma = pltpu.SemaphoreType.DMA
        tile = (chunks, channels, LANES)
        states, tiles = pl.pallas_call(
            functools.partial(kernel, peers, strips),
            out_shape=(
                pltpu.VMEM(guess.shape, f32),
                pltpu.VMEM((layers * 8, LANES), f32),
            ),
            in_specs=[pl.BlockSpec(memory_space=pl.ANY)] * 4,
            out_specs=(pl.BlockSpec(memory_space=pltpu.VMEM), pl.BlockSpec(memory_space=pltpu.VMEM)),
            scratch_shapes=[
                pltpu.VMEM((2, channels, half + 2 * edge), f32),
                pltpu.VMEM((2,) + kernels.shape, kernels.dtype),
                pltpu.VMEM((2,) + biases.shape, biases.dtype),
                pltpu.VMEM((probe_count, channels, half + 2 * edge), bf16),
                pltpu.VMEM((depth, half + 2 * edge), bf16),
                pltpu.VMEM((depth, half), bf16),
                pltpu.VMEM((2, layers * channels, depth), bf16),
                pltpu.VMEM((2, channels, half), f32),
                pltpu.VMEM((2, layers, channels, half), f32),
                pltpu.VMEM((channels, half), f32),
                pltpu.VMEM(tile, f32),
                pltpu.VMEM(tile, f32),
                pltpu.VMEM(tile, f32),
                pltpu.VMEM((2 * layers * 8, LANES), f32),
                pltpu.VMEM((2 * strips - 1, 2 * layers * 8, LANES), f32),
                pltpu.VMEM((8, LANES), f32),
                pltpu.VMEM((8, LANES), f32),
                dma((4,)), dma((3,)), dma((3,)), dma((3,)), dma((3,)), dma((chunks,)), dma((chunks,)),
                dma((chunks,)), dma((chunks,)), dma((2 * strips - 1,)), dma((2 * strips - 1,)), dma((2,)),
            ],
            compiler_params=pltpu.CompilerParams(collective_id=0, has_side_effects=True),
        )(guess, kernels, biases, probes)
        return pl.pallas_call(
            finish,
            out_shape=(
                jax.ShapeDtypeStruct(guess.shape, f32),
                jax.ShapeDtypeStruct((layers,), f32),
            ),
            in_specs=[pl.BlockSpec(memory_space=pltpu.VMEM)] * 2,
            out_specs=(pl.BlockSpec(memory_space=pl.ANY), pl.BlockSpec(memory_space=pltpu.SMEM)),
            scratch_shapes=[dma((4,))],
        )(pltpu.with_memory_space_constraint(states, pltpu.VMEM), pltpu.with_memory_space_constraint(tiles, pltpu.VMEM))

    return jax.shard_map(
        step,
        mesh=mesh,
        in_specs=(
            P("tm", None, None, "space"),
            P("tm", None, None),
            P("tm", None),
            P(None, None, None, "space"),
        ),
        out_specs=(P("tm", None, None, "space"), P("tm")),
        check_vma=False,
    )
```

time: 23.5 us -> 28.2 us (1.20)
  Pallas kernels: 22.7 us -> 27.4 us
    pallas_call x1, Pallas kernels: 21.5 us -> 26.2 us  [step(): pl.pallas_call(functools.partial(kernel, peers, strips), out_shape=(pltpu...]
where the time goes in v3:
time: 28.2 us; the launch traced here: 28 us
  Pallas kernels  27.4 us (97%)
  between operations  0.64 us (2%)
    pallas_call x1, Pallas kernels, step(): pl.pallas_call(functools.partial(kernel, peers, strips), out_shape=(pltpu...  26.2 us
    pallas_call x1, Pallas kernels, step(): pl.pallas_call(finish, out_shape=(jax.ShapeDtypeStruct(guess.shape, f32),...  1.25 us

profile of v3, /device:TPU:24, one launch (start us, length us, event | category | flops | bytes accessed | tf_op | source)
XLA Modules:
  0.0 28.0 jit_solution(2600031700741386711)
XLA Ops:
  0.6 26.2 %shard_map.59 = (f32[1,1,64,1024]{3,2,1,0:T(8,128)S(1)}, f32[16,128]{1,0:T(8,128)S(1)}) custom-call(f32[1,1,64,1024]{3,2,1,0:T(8,128)} %guess_in.1, bf16[2,64,576]{2,1,0:T(8,128)(2,1)} %kernels_in.1, f32[2,64]{1,0:T(2,128)} %biases_in.1, bf16[2,1,64,1024]{3,2,1,0:T(8,128)(2,1)} %probes_in.1), custom_call_target="tpu_custom_call" | custom-call | tf_op jit(solution)/shard_map/pallas_call | solution.py:386
  26.8 1.2 %shard_map.60 = (f32[1,1,64,1024]{3,2,1,0:T(8,128)}, f32[2]{0:T(128)}) custom-call(f32[1,1,64,1024]{3,2,1,0:T(8,128)S(1)} %get-tuple-element.4.states_in, f32[16,128]{1,0:T(8,128)S(1)} %get-tuple-element.5.tiles), custom_call_target="tpu_custom_call" | custom-call | tf_op jit(solution)/shard_map/pallas_call | solution.py:417

commit v4 on v2

--- a/solution.py
+++ b/solution.py
@@ -44,7 +44,7 @@
 
 
 def kernel(peers, strips, guess_in, kernels_in, biases_in, probes_in, states, logs,
-           guess, kernels, biases, probes, load_sem, halo, probe_halo, stack, probe_stack, turned, mine, theirs, own_out, their_off,
+           guess, kernels, biases, probes, load_sem, halo, probe_halo, stack, probe_stack, turned, mine, theirs, own_out, their_off, early_offs, sum_offs,
            chain_in, chain_out, pass_out, trace_out, trace_in, pair_out, pair_in, run_out, run_in,
            halo_send, halo_recv, mat_sem, off_send, off_recv, chain_send, chain_recv,
            pass_send, pass_recv, trace_send, trace_recv, small_sem):
@@ -97,13 +97,19 @@
     probe_down = remote(probes_in.at[:, 0, :, pl.ds(0, edge)], probe_halo.at[1], halo_send.at[3], halo_recv.at[3], k, s - 1)
     has_up, has_down = s < strips - 1, s > 0
 
-    @pl.when(has_up)
+    odd = s % 2 == 1
+
+    @pl.when(jnp.logical_and(has_up, odd))
     def _():
         up.start()
 
     @pl.when(has_down)
     def _():
         down.start()
+
+    @pl.when(jnp.logical_and(has_up, jnp.logical_not(odd)))
+    def _():
+        up.start()
 
     @pl.when(has_up)
     def _():
@@ -227,46 +233,75 @@
     nexts = [remote(chain_out.at[c], chain_in.at[c], chain_send.at[c], chain_recv.at[c], k + 2, s) for c in range(chunks)]
     passes = [remote(pass_out.at[c], states.at[0, 0, :, chunk(x, c)], pass_send.at[c], pass_recv.at[c], partner, s)
               for c in range(chunks)]
+    relays = [remote(chain_in.at[c], states.at[0, 0, :, chunk(x, c)], pass_send.at[c], pass_recv.at[c], partner, s)
+              for c in range(chunks)]
     passed = [remote(pass_out.at[c], states.at[0, 0, :, chunk(1 - x, c)], pass_send.at[c], pass_recv.at[c], partner, s)
               for c in range(chunks)]
     pair = remote(pair_out, pair_in, small_sem.at[0], small_sem.at[1], partner, s)
     onward = remote(run_out, run_in, small_sem.at[2], small_sem.at[3], k + 2, s)
     go_on = q < pairs - 1
     waits = jnp.logical_not(first_pair)
-    for c in range(chunks):
+    def prepare(c):
         offs[c].wait_recv()
         held = own_out[:, chunk(x, c)]
         got = their_off[c]
         early_off = jnp.where(even, held, got)
         late_off = jnp.where(even, got, held)
-        sum_off = late_off + early_off + exact_dot(late_left, early_off)
+        early_offs[c] = early_off
+        sum_offs[c] = late_off + early_off + exact_dot(late_left, early_off)
+
+    def strip_traces():
+        trace_total = trace_out[...]
+        for copy in traces:
+            copy.wait_recv()
+        for d in range(1, strips):
+            trace_total = trace_total + trace_in[d - 1]
+        pair_out[...] = trace_total
+        pair.start()
+
+    @pl.when(q > 0)
+    def _():
+        for c in range(chunks):
+            prepare(c)
+        strip_traces()
+
+    for c in range(chunks):
+        @pl.when(q == 0)
+        def _():
+            prepare(c)
 
         @pl.when(waits)
         def _():
             nexts[c].wait_recv()
 
+        @pl.when(x == 1)
+        def _():
+            relays[c].start()
+
         here = chain_in[c]
         moved = exact_dot(map_left, here)
-        chain_out[c] = here + (moved[0:channels] + sum_off)
+        chain_out[c] = here + (moved[0:channels] + sum_offs[c])
 
         @pl.when(go_on)
         def _():
             nexts[c].start()
 
-        between = here + (moved[channels:2 * channels] + early_off)
-        pass_out[c] = jnp.where(even, between, here)
-        passes[c].start()
+        between = here + (moved[channels:2 * channels] + early_offs[c])
+        pass_out[c] = between
+
+        @pl.when(even)
+        def _():
+            passes[c].start()
+
         states[0, 0, :, chunk(x, c)] = jnp.where(even, here, between)
         if c == max(chunks - 2, 0):
-            trace_total = trace_out[...]
-            for copy in traces:
-                copy.wait_recv()
-            for d in range(1, strips):
-                trace_total = trace_total + trace_in[d - 1]
-            pair_out[...] = trace_total
-            pair.start()
+            @pl.when(q == 0)
+            def _():
+                strip_traces()
 
     pair.wait_recv()
+
+    trace_total = pair_out[...]
 
     def layer_sum(tile):
         result = tile[0:8]
@@ -329,11 +364,16 @@
 
 
 def finish(states_in, tiles, states, logs, sem):
-    copy = pltpu.make_async_copy(states_in, states, sem)
-    copy.start()
+    pieces = sem.shape[0]
+    size = states_in.shape[2] // pieces
+    copies = [pltpu.make_async_copy(states_in.at[:, :, pl.ds(i * size, size)], states.at[:, :, pl.ds(i * size, size)], sem.at[i])
+              for i in range(pieces)]
+    for copy in copies:
+        copy.start()
     for n in range(logs.shape[0]):
         logs[n] = jnp.sum(tiles[n * 8:(n + 1) * 8])
-    copy.wait()
+    for copy in copies:
+        copy.wait()
 
 
 def solution(mesh):
@@ -374,6 +414,8 @@
                 pltpu.VMEM(tile, f32),
                 pltpu.VMEM(tile, f32),
                 pltpu.VMEM(tile, f32),
+                pltpu.VMEM(tile, f32),
+                pltpu.VMEM(tile, f32),
                 pltpu.VMEM((layers * 8, LANES), f32),
                 pltpu.VMEM((max(strips - 1, 1), layers * 8, LANES), f32),
                 pltpu.VMEM((layers * 8, LANES), f32),
@@ -393,7 +435,7 @@
             ),
             in_specs=[pl.BlockSpec(memory_space=pltpu.VMEM)] * 2,
             out_specs=(pl.BlockSpec(memory_space=pl.ANY), pl.BlockSpec(memory_space=pltpu.SMEM)),
-            scratch_shapes=[dma],
+            scratch_shapes=[dma((4,))],
         )(pltpu.with_memory_space_constraint(states, pltpu.VMEM), pltpu.with_memory_space_constraint(tiles, pltpu.VMEM))
 
     return jax.shard_map(

time: 23.5 us -> 23.2 us (0.987)
  Pallas kernels: 22.7 us -> 22.4 us
    pallas_call x1, Pallas kernels: 21.5 us -> 21.2 us  [step(): pl.pallas_call(functools.partial(kernel, peers, strips), out_shape=(pltpu...]
where the time goes in v4:
time: 23.2 us; the launch traced here: 23.1 us
  Pallas kernels  22.4 us (97%)
  between operations  0.64 us (3%)
    pallas_call x1, Pallas kernels, step(): pl.pallas_call(functools.partial(kernel, peers, strips), out_shape=(pltpu...  21.2 us
    pallas_call x1, Pallas kernels, step(): pl.pallas_call(finish, out_shape=(jax.ShapeDtypeStruct(guess.shape, f32),...  1.25 us

profile of v4, /device:TPU:24, one launch (start us, length us, event | category | flops | bytes accessed | tf_op | source)
XLA Modules:
  0.0 23.1 jit_solution(9490811175090171418)
XLA Ops:
  0.6 21.2 %shard_map.59 = (f32[1,1,64,1024]{3,2,1,0:T(8,128)S(1)}, f32[16,128]{1,0:T(8,128)S(1)}) custom-call(f32[1,1,64,1024]{3,2,1,0:T(8,128)} %guess_in.1, bf16[2,64,576]{2,1,0:T(8,128)(2,1)} %kernels_in.1, f32[2,64]{1,0:T(2,128)} %biases_in.1, bf16[2,1,64,1024]{3,2,1,0:T(8,128)(2,1)} %probes_in.1), custom_call_target="tpu_custom_call" | custom-call | tf_op jit(solution)/shard_map/pallas_call | solution.py:391
  21.8 1.2 %shard_map.60 = (f32[1,1,64,1024]{3,2,1,0:T(8,128)}, f32[2]{0:T(128)}) custom-call(f32[1,1,64,1024]{3,2,1,0:T(8,128)S(1)} %get-tuple-element.4.states_in, f32[16,128]{1,0:T(8,128)S(1)} %get-tuple-element.5.tiles), custom_call_target="tpu_custom_call" | custom-call | tf_op jit(solution)/shard_map/pallas_call | solution.py:430
